TPU v7x, 32 devices: a whole 2x2x4 slice. The times are simulated.
32 devices in a mesh: space: 4 (over z), energy: 8 (over y, x, core).
Axes of the slice: x: 2, y: 2, z: 4, core: 2. Of those that a mesh axis runs over, the one named last changes fastest.
Arguments:
- retain: float32 [8, 8], P('space', 'energy'), may hold values from 0.12 to 0.89
- hopping: float32 [8, 8, 2, 128, 128], P('space', 'energy'), may hold values from -0.125 to 0.125
- source: float32 [8, 8, 2, 128, 128], P('space', 'energy'), may hold values from -0.9 to 0.9
- screened: float32 [8, 8, 2, 16384], P('space', None, None, 'energy'), may hold values from -2 to 2
Outputs:
- greens: float32 [8, 8, 2, 128, 128], P('space', 'energy')
- self_energy: float32 [8, 8, 2, 16384], P('space', None, None, 'energy')
All inputs are finite; a program needn't handle non-finite values.
Results may differ from a plain program's by a relative error of at most 0.0001.
Values sent between devices are 32-bit elements; how exact they have to be, the bound alone decides.
A program may use at most 64 MiB of HBM per device.

v0:
```python
import math
import jax
import jax.numpy as jnp
from jax import lax
from jax.sharding import PartitionSpec as P

EXACT_PRECISION = lax.Precision.HIGHEST


def shifted(value, axis, steps):
    count = lax.axis_size(axis)
    initial, last = (max(0, -steps), min(count, count - steps))
    return lax.ppermute(value, axis, [(source, source + steps) for source in range(initial, last)])


def build_coupler(retain_slab, hop_slab):
    size = hop_slab.shape[-1]
    diagonal_ones = jnp.eye(size, dtype=jnp.float32)
    factor = retain_slab[:, None, None]
    return jnp.stack([factor * (diagonal_ones + hop_slab[:, 0]), factor * hop_slab[:, 1]], axis=1)


def complex_product(left_matrix, right_matrix):
    real_component = jnp.einsum(
        "eij,ejk->eik", left_matrix[:, 0], right_matrix[:, 0], precision=EXACT_PRECISION
    ) - jnp.einsum("eij,ejk->eik", left_matrix[:, 1], right_matrix[:, 1], precision=EXACT_PRECISION)
    imaginary_component = jnp.einsum(
        "eij,ejk->eik", left_matrix[:, 0], right_matrix[:, 1], precision=EXACT_PRECISION
    ) + jnp.einsum("eij,ejk->eik", left_matrix[:, 1], right_matrix[:, 0], precision=EXACT_PRECISION)
    return jnp.stack([real_component, imaginary_component], axis=1)


def times_dagger(left_matrix, right_matrix):
    real_component = jnp.einsum(
        "eij,ekj->eik", left_matrix[:, 0], right_matrix[:, 0], precision=EXACT_PRECISION
    ) + jnp.einsum("eij,ekj->eik", left_matrix[:, 1], right_matrix[:, 1], precision=EXACT_PRECISION)
    imaginary_component = jnp.einsum(
        "eij,ekj->eik", left_matrix[:, 1], right_matrix[:, 0], precision=EXACT_PRECISION
    ) - jnp.einsum("eij,ekj->eik", left_matrix[:, 0], right_matrix[:, 1], precision=EXACT_PRECISION)
    return jnp.stack([real_component, imaginary_component], axis=1)


def sandwich(coupler, middle):
    return times_dagger(complex_product(coupler, middle), coupler)


def fourier_tables(length, columns):
    rows_index = jnp.arange(length, dtype=jnp.int32)[:, None]
    cols_index = jnp.arange(columns, dtype=jnp.int32)[None, :]
    phases = (rows_index * cols_index % length).astype(jnp.float32) * (2.0 * math.pi / length)
    return (jnp.cos(phases), jnp.sin(phases))


def forward_transform(series, cosine_lookup, sine_lookup):
    real_input = series[:, :, 0]
    imaginary_input = series[:, :, 1]
    real_component = jnp.einsum(
        "gt,itx->igx", cosine_lookup, real_input, precision=EXACT_PRECISION
    ) + jnp.einsum("gt,itx->igx", sine_lookup, imaginary_input, precision=EXACT_PRECISION)
    imaginary_component = jnp.einsum(
        "gt,itx->igx", cosine_lookup, imaginary_input, precision=EXACT_PRECISION
    ) - jnp.einsum("gt,itx->igx", sine_lookup, real_input, precision=EXACT_PRECISION)
    return jnp.stack([real_component, imaginary_component], axis=2)


def body(retain, hopping, source, screened):
    couplers = jax.vmap(build_coupler)(retain, hopping)

    def compose_step(running, slab_data):
        total_map, total_source = running
        coupler, fresh_source = slab_data
        return (
            (complex_product(coupler, total_map), sandwich(coupler, total_source) + fresh_source),
            None,
        )

    (device_map, device_source), _ = lax.scan(
        compose_step, (couplers[0], source[0]), (couplers[1:], source[1:])
    )

    def hand_over(counter, arriving):
        leaving = sandwich(device_map, arriving) + device_source
        return shifted(leaving, "space", 1)

    entering = lax.fori_loop(
        0, lax.axis_size("space") - 1, hand_over, jnp.zeros_like(device_source)
    )

    def apply_step(arriving, slab_data):
        coupler, fresh_source = slab_data
        leaving = sandwich(coupler, arriving) + fresh_source
        return (leaving, leaving)

    _, greens = lax.scan(apply_step, entering, (couplers, source))
    pair_blocks = greens.reshape(
        greens.shape[0], greens.shape[1], 2, greens.shape[3] * greens.shape[4]
    )
    total_energies = greens.shape[1] * lax.axis_size("energy")
    period = 2 * total_energies
    cosine_lookup, sine_lookup = fourier_tables(period, total_energies)
    green_spectrum = forward_transform(
        lax.all_to_all(pair_blocks, "energy", split_axis=3, concat_axis=1, tiled=True),
        cosine_lookup,
        sine_lookup,
    )
    screen_spectrum = forward_transform(screened, cosine_lookup, sine_lookup)
    real_result = (
        green_spectrum[:, :, 0] * screen_spectrum[:, :, 0]
        - green_spectrum[:, :, 1] * screen_spectrum[:, :, 1]
    )
    imaginary_result = (
        green_spectrum[:, :, 0] * screen_spectrum[:, :, 1]
        + green_spectrum[:, :, 1] * screen_spectrum[:, :, 0]
    )
    real_component = (
        jnp.einsum("wo,cwd->cod", cosine_lookup, real_result, precision=EXACT_PRECISION)
        - jnp.einsum("wo,cwd->cod", sine_lookup, imaginary_result, precision=EXACT_PRECISION)
    ) / period
    imaginary_component = (
        jnp.einsum("wo,cwd->cod", cosine_lookup, imaginary_result, precision=EXACT_PRECISION)
        + jnp.einsum("wo,cwd->cod", sine_lookup, real_result, precision=EXACT_PRECISION)
    ) / period
    self_energy = jnp.stack([real_component, imaginary_component], axis=2)
    return (greens, self_energy)


def solution(mesh):
    placed = (
        P("space", "energy"),
        P("space", "energy", None, None, None),
        P("space", "energy", None, None, None),
        P("space", None, None, "energy"),
    )
    return jax.shard_map(
        body,
        mesh=mesh,
        in_specs=placed,
        out_specs=(P("space", "energy", None, None, None), P("space", None, None, "energy")),
        check_vma=False,
    )
```

profile of v0, /device:TPU:0, one launch (start us, length us, event | category | flops | bytes accessed | tf_op | source)
XLA Modules:
  0.0 140.6 jit_solution(247373426349361048)
XLA Ops:
  0.6 1.1 slice_multiply_fusion
  1.7 0.9 fusion.56
  5.5 0.9 maximum_add_fusion.3
  6.4 27.3 %while.8 = (s32[]{:T(128)}, f32[1,2,128,128]{3,2,1,0:T(8,128)S(1)}, f32[1,2,128,128]{3,2,1,0:T(8,128)S(1)}, f32[1,2,128,128]{3,2,1,0:T(8,128)S(1)}, s32[]{:T(128)}) while((s32[]{:T(128)}, f32[1,2,128,128]{3,2,1,0:T(8,128)S(1)}, f32[1,2,128,128]{3,2,1,0:T(8,128)S(1)}, f32[1,2,128,128]{3,2,1,0:T(8,128)S(1)}, s32[]{:T(128)}) %tuple.44), condition=%wide.region_1.2_spmd, body=%wide.region_0.1_spmd.sunk | while | flops 201457664 | bytes 2752613 | solution.py:85
  8.4 5.0 %collective-permute-start = (f32[1,2,128,128]{3,2,1,0:T(8,128)S(1)}, f32[1,2,128,128]{3,2,1,0:T(8,128)S(1)}, u32[]{:S(2)}, u32[]{:S(2)}) collective-permute-start(f32[1,2,128,128]{3,2,1,0:T(8,128)S(1)} %maximum_add_fusion.6), channel_id=1, source_target_pairs={{0,8},{8,16},{16,24},{1,9},{9,17},{17,25},{2,10},{10,18},{18,26},{... | collective-permute-start | bytes 393224 | tf_op jit(solution)/shard_map/while/body/eval_jaxpr/ppermute | solution.py:13
  13.4 2.7 %collective-permute-done = f32[1,2,128,128]{3,2,1,0:T(8,128)S(1)} collective-permute-done((f32[1,2,128,128]{3,2,1,0:T(8,128)S(1)}, f32[1,2,128,128]{3,2,1,0:T(8,128)S(1)}, u32[]{:S(2)}, u32[]{:S(2)}) %collective-permute-start) | collective-permute-done | bytes 131104 | tf_op jit(solution)/shard_map/while/body/eval_jaxpr/ppermute | solution.py:13
  18.0 4.4 %collective-permute-start = (f32[1,2,128,128]{3,2,1,0:T(8,128)S(1)}, f32[1,2,128,128]{3,2,1,0:T(8,128)S(1)}, u32[]{:S(2)}, u32[]{:S(2)}) collective-permute-start(f32[1,2,128,128]{3,2,1,0:T(8,128)S(1)} %maximum_add_fusion.6), channel_id=1, source_target_pairs={{0,8},{8,16},{16,24},{1,9},{9,17},{17,25},{2,10},{10,18},{18,26},{... | collective-permute-start | bytes 393224 | tf_op jit(solution)/shard_map/while/body/eval_jaxpr/ppermute | solution.py:13
  22.4 2.5 %collective-permute-done = f32[1,2,128,128]{3,2,1,0:T(8,128)S(1)} collective-permute-done((f32[1,2,128,128]{3,2,1,0:T(8,128)S(1)}, f32[1,2,128,128]{3,2,1,0:T(8,128)S(1)}, u32[]{:S(2)}, u32[]{:S(2)}) %collective-permute-start) | collective-permute-done | bytes 131104 | tf_op jit(solution)/shard_map/while/body/eval_jaxpr/ppermute | solution.py:13
  26.9 4.4 %collective-permute-start = (f32[1,2,128,128]{3,2,1,0:T(8,128)S(1)}, f32[1,2,128,128]{3,2,1,0:T(8,128)S(1)}, u32[]{:S(2)}, u32[]{:S(2)}) collective-permute-start(f32[1,2,128,128]{3,2,1,0:T(8,128)S(1)} %maximum_add_fusion.6), channel_id=1, source_target_pairs={{0,8},{8,16},{16,24},{1,9},{9,17},{17,25},{2,10},{10,18},{18,26},{... | collective-permute-start | bytes 393224 | tf_op jit(solution)/shard_map/while/body/eval_jaxpr/ppermute | solution.py:13
  31.2 2.5 %collective-permute-done = f32[1,2,128,128]{3,2,1,0:T(8,128)S(1)} collective-permute-done((f32[1,2,128,128]{3,2,1,0:T(8,128)S(1)}, f32[1,2,128,128]{3,2,1,0:T(8,128)S(1)}, u32[]{:S(2)}, u32[]{:S(2)}) %collective-permute-start) | collective-permute-done | bytes 131104 | tf_op jit(solution)/shard_map/while/body/eval_jaxpr/ppermute | solution.py:13
  33.7 7.6 %while.28 = (s32[]{:T(128)}, f32[1,2,128,128]{3,2,1,0:T(8,128)S(1)}, f32[2,1,2,128,128]{4,3,2,1,0:T(8,128)S(1)}, f32[2,1,2,128,128]{4,3,2,1,0:T(8,128)S(1)}, f32[2,1,2,128,128]{4,3,2,1,0:T(8,128)}, /*index=5*/s32[]{:T(128)}) while((s32[]{:T(128)}, f32[1,2,128,128]{3,2,1,0:T(8,128)S(1)}, f32[2,1,2,128,128]{4,3,2,1,0:T(8,128)S(1)}, ...), condition=%wide.region_3.4_spmd, body=%wide.region_2.3_spmd.sunk | while | flops 201523200 | bytes 2883665 | solution.py:94
  35.7 0.9 fusion.238
  36.6 0.9 maximum_add_fusion.7
  39.5 0.9 fusion.238
  40.4 0.9 maximum_add_fusion.7
  41.4 11.3 %copy.10 = f32[2,1,2,128,128]{0,2,4,3,1:T(2,128)} copy(f32[2,1,2,128,128]{4,3,2,1,0:T(8,128)S(1)} %get-tuple-element.70) | data formatting | bytes 524288 | tf_op jit(solution)/shard_map/while | solution.py:94
  52.7 25.8 %reshape.358 = f32[8,1,8192]{2,1,0:T(1,128)} reshape(f32[16384,1,2,2]{3,2,1,0:T(2,128)} %bitcast.277) | data formatting | bytes 524288
  78.6 3.7 %all-to-all-start = ((f32[8,1,8192]{2,1,0:T(1,128)}), f32[8,1,8192]{2,1,0:T(1,128)S(1)}, u32[]{:S(2)}, u32[]{:S(2)}) async-start(f32[8,1,8192]{2,1,0:T(1,128)} %reshape.358), calls=%async_computation | async-start | bytes 524288 | tf_op jit(solution)/shard_map/all_to_all | solution.py:102
  84.4 4.8 %all-to-all-done = f32[8,1,8192]{2,1,0:T(1,128)S(1)} async-done(((f32[8,1,8192]{2,1,0:T(1,128)}), f32[8,1,8192]{2,1,0:T(1,128)S(1)}, u32[]{:S(2)}, u32[]{:S(2)}) %all-to-all-start) | async-done | bytes 262176 | tf_op jit(solution)/shard_map/all_to_all | solution.py:102
  89.7 1.3 reduce
  91.0 32.2 %reshape.359 = f32[16384,1,2,2]{3,2,1,0:T(2,128)} reshape(f32[8,8192]{1,0:T(8,128)S(1)} %reduce) | data formatting | bytes 524288
  123.1 13.4 %copy.15 = f32[2,1,2,8,2048]{4,3,0,2,1:T(8,128)S(1)} copy(f32[2,1,2,8,2048]{0,2,4,3,1:T(2,128)} %bitcast.276) | data formatting | bytes 524288 | tf_op jit(solution)/shard_map/all_to_all | solution.py:102
  138.0 0.5 multiply_subtract_fusion
  139.7 0.9 copy.14
  (80 shorter events, 17.5 us)
Async XLA Ops:
  8.4 7.7 %collective-permute-start = (f32[1,2,128,128]{3,2,1,0:T(8,128)S(1)}, f32[1,2,128,128]{3,2,1,0:T(8,128)S(1)}, u32[]{:S(2)}, u32[]{:S(2)}) collective-permute-start(f32[1,2,128,128]{3,2,1,0:T(8,128)S(1)} %maximum_add_fusion.6), channel_id=1, source_target_pairs={{0,8},{8,16},{16,24},{1,9},{9,17},{17,25},{2,10},{10,18},{18,26},{... | collective-permute-start | bytes 393224 | tf_op jit(solution)/shard_map/while/body/eval_jaxpr/ppermute | solution.py:13
  18.0 6.9 %collective-permute-start = (f32[1,2,128,128]{3,2,1,0:T(8,128)S(1)}, f32[1,2,128,128]{3,2,1,0:T(8,128)S(1)}, u32[]{:S(2)}, u32[]{:S(2)}) collective-permute-start(f32[1,2,128,128]{3,2,1,0:T(8,128)S(1)} %maximum_add_fusion.6), channel_id=1, source_target_pairs={{0,8},{8,16},{16,24},{1,9},{9,17},{17,25},{2,10},{10,18},{18,26},{... | collective-permute-start | bytes 393224 | tf_op jit(solution)/shard_map/while/body/eval_jaxpr/ppermute | solution.py:13
  26.9 6.9 %collective-permute-start = (f32[1,2,128,128]{3,2,1,0:T(8,128)S(1)}, f32[1,2,128,128]{3,2,1,0:T(8,128)S(1)}, u32[]{:S(2)}, u32[]{:S(2)}) collective-permute-start(f32[1,2,128,128]{3,2,1,0:T(8,128)S(1)} %maximum_add_fusion.6), channel_id=1, source_target_pairs={{0,8},{8,16},{16,24},{1,9},{9,17},{17,25},{2,10},{10,18},{18,26},{... | collective-permute-start | bytes 393224 | tf_op jit(solution)/shard_map/while/body/eval_jaxpr/ppermute | solution.py:13
  41.4 37.2 %copy-start = (f32[2,1,2,128,128]{4,3,2,1,0:T(8,128)}, f32[2,1,2,128,128]{4,3,2,1,0:T(8,128)S(1)}, u32[]{:S(2)}) copy-start(f32[2,1,2,128,128]{4,3,2,1,0:T(8,128)S(1)} %get-tuple-element.70) | copy-start | bytes 786436
  41.4 40.9 %copy-start.1 = (f32[2,8,2,2048]{3,2,1,0:T(2,128)S(1)}, f32[2,8,2,2048]{3,2,1,0:T(2,128)}, u32[]{:S(2)}) copy-start(f32[2,8,2,2048]{3,2,1,0:T(2,128)} %param.11) | copy-start | bytes 786436
  78.6 10.6 %all-to-all-start = ((f32[8,1,8192]{2,1,0:T(1,128)}), f32[8,1,8192]{2,1,0:T(1,128)S(1)}, u32[]{:S(2)}, u32[]{:S(2)}) async-start(f32[8,1,8192]{2,1,0:T(1,128)} %reshape.358), calls=%async_computation | async-start | bytes 524288 | tf_op jit(solution)/shard_map/all_to_all | solution.py:102
where the time goes:
time: 141 us
  local copies, waits for them, and re-layouts  84.4 us (60%)
  starting transfers between devices  17.4 us (12%)
  matrix products  17.2 us (12%)
  waiting for transfers between devices  12.5 us (9%)
  other arithmetic  7.99 us (6%)
    unnamed x7, local copies, waits for them, and re-layouts  58.9 us
    all_to_all x2, local copies, waits for them, and re-layouts, body(): lax.all_to_all(pair_blocks, 'energy', split_axis=3, concat_axis=1, tiled=...  13.9 us
    ppermute x3, starting transfers between devices, shifted(): lax.ppermute(value, axis, [(source, source + steps) for source in range(i...  13.7 us
    while x1, local copies, waits for them, and re-layouts, body(): _, greens = lax.scan(apply_step, entering, (couplers, source))  11.3 us
    ppermute x3, waiting for transfers between devices, shifted(): lax.ppermute(value, axis, [(source, source + steps) for source in range(i...  7.72 us
    all_to_all x1, waiting for transfers between devices, body(): lax.all_to_all(pair_blocks, 'energy', split_axis=3, concat_axis=1, tiled=...  4.77 us
    all_to_all x1, starting transfers between devices, body(): lax.all_to_all(pair_blocks, 'energy', split_axis=3, concat_axis=1, tiled=...  3.72 us
  transfers between devices with their start and end apart: 4, of which 4 were waited for; matrix products, arithmetic and copies ran while one was open for 1% of the time, Pallas kernels for 0%

commit v1 on v0

--- a/solution.py
+++ b/solution.py
@@ -5,6 +5,13 @@
 from jax.sharding import PartitionSpec as P
 
 EXACT_PRECISION = lax.Precision.HIGHEST
+
+
+def trade_parts(x, axis, split, join):
+    size = lax.axis_size(axis)
+    blocks = jnp.stack(jnp.split(x, size, axis=split), axis=0)
+    blocks = lax.all_to_all(blocks, axis, split_axis=0, concat_axis=0)
+    return jnp.concatenate(blocks, axis=join)
 
 
 def shifted(value, axis, steps):
@@ -99,9 +106,7 @@
     period = 2 * total_energies
     cosine_lookup, sine_lookup = fourier_tables(period, total_energies)
     green_spectrum = forward_transform(
-        lax.all_to_all(pair_blocks, "energy", split_axis=3, concat_axis=1, tiled=True),
-        cosine_lookup,
-        sine_lookup,
+        trade_parts(pair_blocks, "energy", 3, 1), cosine_lookup, sine_lookup
     )
     screen_spectrum = forward_transform(screened, cosine_lookup, sine_lookup)
     real_result = (

time: 141 us -> 57.8 us (0.41)
  local copies, waits for them, and re-layouts: 84.4 us -> 7.79 us
  other arithmetic: 7.99 us -> 1.33 us
    unnamed x7 -> x16, local copies, waits for them, and re-layouts: 58.9 us -> 6.59 us
    all_to_all x2 -> x1, local copies, waits for them, and re-layouts: 13.9 us -> 0.16 us  [trade_parts(): blocks = lax.all_to_all(blocks, axis, split_axis=0, concat_axis=0)]
    while x1 -> x0, local copies, waits for them, and re-layouts: 11.3 us -> none  [body(): _, greens = lax.scan(apply_step, entering, (couplers, source))]
    add x2, other arithmetic: 1.85 us -> 0.03 us  [apply_step(): leaving = sandwich(coupler, arriving) + fresh_source]
    dynamic_update_slice x2, other arithmetic: 1.85 us -> 0.04 us  [body(): _, greens = lax.scan(apply_step, entering, (couplers, source))]
  transfers between devices with their start and end apart: 4 -> 4, of which waited for: 4 -> 4; matrix products, arithmetic and copies ran while one was open for 1% -> 4% of each run, Pallas kernels for 0% -> 0%
where the time goes in v1:
time: 57.8 us; the launch traced here: 57.5 us
  starting transfers between devices  17.6 us (30%)
  matrix products  17.1 us (30%)
  waiting for transfers between devices  12.5 us (22%)
  local copies, waits for them, and re-layouts  7.79 us (13%)
  other arithmetic  1.33 us (2%)
  between operations  0.92 us (2%)
    ppermute x3, starting transfers between devices, shifted(): lax.ppermute(value, axis, [(source, source + steps) for source in range(i...  13.7 us
    ppermute x3, waiting for transfers between devices, shifted(): lax.ppermute(value, axis, [(source, source + steps) for source in range(i...  7.71 us
    unnamed x16, local copies, waits for them, and re-layouts  6.59 us
    all_to_all x1, waiting for transfers between devices, trade_parts(): blocks = lax.all_to_all(blocks, axis, split_axis=0, concat_axis=0)  4.77 us
    all_to_all x1, starting transfers between devices, trade_parts(): blocks = lax.all_to_all(blocks, axis, split_axis=0, concat_axis=0)  3.86 us
    dot_general x6, matrix products, times_dagger(): jnp.einsum('eij,ekj->eik', left_matrix[:, 1], right_matrix[:, 1], precisi...  1.62 us
    dot_general x6, matrix products, times_dagger(): jnp.einsum('eij,ekj->eik', left_matrix[:, 0], right_matrix[:, 1], precisi...  1.61 us
    dot_general x6, matrix products, times_dagger(): jnp.einsum('eij,ekj->eik', left_matrix[:, 0], right_matrix[:, 0], precisi...  1.6 us
  transfers between devices with their start and end apart: 4, of which 4 were waited for; matrix products, arithmetic and copies ran while one was open for 4% of the time, Pallas kernels for 0%

profile of v1, /device:TPU:0, one launch (start us, length us, event | category | flops | bytes accessed | tf_op | source)
XLA Modules:
  0.0 57.5 jit_solution(1096530413958129201)
XLA Ops:
  0.7 0.6 %copy-done.3 = f32[2,1]{0,1:T(1,128)S(1)} copy-done((f32[2,1]{0,1:T(1,128)S(1)}, f32[2,1]{0,1:T(1,128)}, u32[]{:S(2)}) %copy-start.3) | copy-done | bytes 32
  1.3 1.1 %slice_multiply_fusion = (f32[2,1,1,128,128]{4,3,2,1,0:T(8,128)S(1)}, f32[2,1,1,128,128]{4,3,2,1,0:T(8,128)S(1)}) fusion(f32[2,1,2,128,128]{4,3,2,1,0:T(8,128)} %param.9, f32[2]{0:T(128)S(1)} %bitcast.316, f32[128,128]{1,0:T(8,128)S(1)} %fusion.63), kind=kLoop, calls=%fused_computation.101 | loop fusion | flops 98304 | bytes 589832 | tf_op jit(solution)/shard_map/vmap()/mul | solution.py:27
  5.3 27.3 %while.8 = (s32[]{:T(128)}, f32[1,2,128,128]{3,2,1,0:T(8,128)S(1)}, f32[1,2,128,128]{3,2,1,0:T(8,128)S(1)}, f32[1,2,128,128]{3,2,1,0:T(8,128)S(1)}, s32[]{:T(128)}) while((s32[]{:T(128)}, f32[1,2,128,128]{3,2,1,0:T(8,128)S(1)}, f32[1,2,128,128]{3,2,1,0:T(8,128)S(1)}, f32[1,2,128,128]{3,2,1,0:T(8,128)S(1)}, s32[]{:T(128)}) %tuple.51), condition=%wide.region_1.2_spmd, body=%wide.region_0.1_spmd.sunk | while | flops 201457664 | bytes 2752613 | solution.py:92
  7.3 5.0 %collective-permute-start = (f32[1,2,128,128]{3,2,1,0:T(8,128)S(1)}, f32[1,2,128,128]{3,2,1,0:T(8,128)S(1)}, u32[]{:S(2)}, u32[]{:S(2)}) collective-permute-start(f32[1,2,128,128]{3,2,1,0:T(8,128)S(1)} %maximum_add_fusion.6), channel_id=1, source_target_pairs={{0,8},{8,16},{16,24},{1,9},{9,17},{17,25},{2,10},{10,18},{18,26},{... | collective-permute-start | bytes 393224 | tf_op jit(solution)/shard_map/while/body/eval_jaxpr/ppermute | solution.py:20
  12.3 2.7 %collective-permute-done = f32[1,2,128,128]{3,2,1,0:T(8,128)S(1)} collective-permute-done((f32[1,2,128,128]{3,2,1,0:T(8,128)S(1)}, f32[1,2,128,128]{3,2,1,0:T(8,128)S(1)}, u32[]{:S(2)}, u32[]{:S(2)}) %collective-permute-start) | collective-permute-done | bytes 131104 | tf_op jit(solution)/shard_map/while/body/eval_jaxpr/ppermute | solution.py:20
  16.9 4.4 %collective-permute-start = (f32[1,2,128,128]{3,2,1,0:T(8,128)S(1)}, f32[1,2,128,128]{3,2,1,0:T(8,128)S(1)}, u32[]{:S(2)}, u32[]{:S(2)}) collective-permute-start(f32[1,2,128,128]{3,2,1,0:T(8,128)S(1)} %maximum_add_fusion.6), channel_id=1, source_target_pairs={{0,8},{8,16},{16,24},{1,9},{9,17},{17,25},{2,10},{10,18},{18,26},{... | collective-permute-start | bytes 393224 | tf_op jit(solution)/shard_map/while/body/eval_jaxpr/ppermute | solution.py:20
  21.3 2.5 %collective-permute-done = f32[1,2,128,128]{3,2,1,0:T(8,128)S(1)} collective-permute-done((f32[1,2,128,128]{3,2,1,0:T(8,128)S(1)}, f32[1,2,128,128]{3,2,1,0:T(8,128)S(1)}, u32[]{:S(2)}, u32[]{:S(2)}) %collective-permute-start) | collective-permute-done | bytes 131104 | tf_op jit(solution)/shard_map/while/body/eval_jaxpr/ppermute | solution.py:20
  25.8 4.4 %collective-permute-start = (f32[1,2,128,128]{3,2,1,0:T(8,128)S(1)}, f32[1,2,128,128]{3,2,1,0:T(8,128)S(1)}, u32[]{:S(2)}, u32[]{:S(2)}) collective-permute-start(f32[1,2,128,128]{3,2,1,0:T(8,128)S(1)} %maximum_add_fusion.6), channel_id=1, source_target_pairs={{0,8},{8,16},{16,24},{1,9},{9,17},{17,25},{2,10},{10,18},{18,26},{... | collective-permute-start | bytes 393224 | tf_op jit(solution)/shard_map/while/body/eval_jaxpr/ppermute | solution.py:20
  30.1 2.5 %collective-permute-done = f32[1,2,128,128]{3,2,1,0:T(8,128)S(1)} collective-permute-done((f32[1,2,128,128]{3,2,1,0:T(8,128)S(1)}, f32[1,2,128,128]{3,2,1,0:T(8,128)S(1)}, u32[]{:S(2)}, u32[]{:S(2)}) %collective-permute-start) | collective-permute-done | bytes 131104 | tf_op jit(solution)/shard_map/while/body/eval_jaxpr/ppermute | solution.py:20
  32.6 4.0 %while.28 = (s32[]{:T(128)}, f32[1,2,128,128]{3,2,1,0:T(8,128)S(1)}, f32[2,1,2,128,128]{4,3,2,1,0:T(8,128)S(1)}, f32[2,1,2,128,128]{4,3,2,1,0:T(8,128)S(1)}, f32[2,1,2,128,128]{4,3,2,1,0:T(8,128)S(1)}, /*index=5*/s32[]{:T(128)}) while((s32[]{:T(128)}, f32[1,2,128,128]{3,2,1,0:T(8,128)S(1)}, f32[2,1,2,128,128]{4,3,2,1,0:T(8,128)S(1)}, ...), condition=%wide.region_3.4_spmd, body=%wide.region_2.3_spmd.sunk | while | flops 201523200 | bytes 2883673 | solution.py:101
  36.8 0.5 copy-done.2
  37.4 0.6 %fusion.77 = f32[8,2,1,2,2048]{4,1,3,2,0:T(2,128)} fusion(f32[2,1,2,2048]{3,2,0,1:T(2,128)S(1)} %get-tuple-element.103), kind=kLoop, calls=%fused_computation.136 | loop fusion | bytes 65536
  38.0 0.6 %fusion.76 = f32[8,2,1,2,2048]{4,1,3,2,0:T(2,128)} fusion(f32[8,2,1,2,2048]{4,1,3,2,0:T(2,128)} %fusion.77, f32[2,1,2,2048]{3,2,0,1:T(2,128)S(1)} %get-tuple-element.102), kind=kLoop, calls=%fused_computation.134 | loop fusion | bytes 65536
  38.7 0.6 %fusion.75 = f32[8,2,1,2,2048]{4,1,3,2,0:T(2,128)} fusion(f32[8,2,1,2,2048]{4,1,3,2,0:T(2,128)} %fusion.76, f32[2,1,2,2048]{3,2,0,1:T(2,128)S(1)} %get-tuple-element.101), kind=kLoop, calls=%fused_computation.132 | loop fusion | bytes 65536
  39.3 0.6 %fusion.74 = f32[8,2,1,2,2048]{4,1,3,2,0:T(2,128)} fusion(f32[8,2,1,2,2048]{4,1,3,2,0:T(2,128)} %fusion.75, f32[2,1,2,2048]{3,2,0,1:T(2,128)S(1)} %get-tuple-element.100), kind=kLoop, calls=%fused_computation.130 | loop fusion | bytes 65536
  39.9 0.6 %fusion.73 = f32[8,2,1,2,2048]{4,1,3,2,0:T(2,128)} fusion(f32[8,2,1,2,2048]{4,1,3,2,0:T(2,128)} %fusion.74, f32[2,1,2,2048]{3,2,0,1:T(2,128)S(1)} %get-tuple-element.99), kind=kLoop, calls=%fused_computation.128 | loop fusion | bytes 65536
  40.6 0.6 %fusion.72 = f32[8,2,1,2,2048]{4,1,3,2,0:T(2,128)} fusion(f32[8,2,1,2,2048]{4,1,3,2,0:T(2,128)} %fusion.73, f32[2,1,2,2048]{3,2,0,1:T(2,128)S(1)} %get-tuple-element.98), kind=kLoop, calls=%fused_computation.126 | loop fusion | bytes 65536
  41.2 0.6 %fusion.71 = f32[8,2,1,2,2048]{4,1,3,2,0:T(2,128)} fusion(f32[8,2,1,2,2048]{4,1,3,2,0:T(2,128)} %fusion.72, f32[2,1,2,2048]{3,2,0,1:T(2,128)S(1)} %get-tuple-element.97), kind=kLoop, calls=%fused_computation.124 | loop fusion | bytes 65536
  41.9 0.6 %fusion.70 = f32[8,2,1,2,2048]{4,1,3,2,0:T(2,128)} fusion(f32[8,2,1,2,2048]{4,1,3,2,0:T(2,128)} %fusion.71, f32[2,1,2,2048]{3,2,0,1:T(2,128)S(1)} %get-tuple-element.96), kind=kLoop, calls=%fused_computation.122 | loop fusion | bytes 65536 | tf_op jit(solution)/shard_map/stack | solution.py:12
  42.5 3.9 %all-to-all-start = ((f32[8,2,1,2,2048]{4,1,3,2,0:T(2,128)}), f32[8,2,1,2,2048]{4,1,3,2,0:T(2,128)S(1)}, u32[]{:S(2)}, u32[]{:S(2)}) async-start(f32[8,2,1,2,2048]{4,1,3,2,0:T(2,128)} %fusion.70), calls=%async_computation | async-start | bytes 524288 | tf_op jit(solution)/shard_map/all_to_all | solution.py:13
  47.5 0.5 fusion.43
  48.5 4.8 %all-to-all-done = f32[8,2,1,2,2048]{4,1,3,2,0:T(2,128)S(1)} async-done(((f32[8,2,1,2,2048]{4,1,3,2,0:T(2,128)}), f32[8,2,1,2,2048]{4,1,3,2,0:T(2,128)S(1)}, u32[]{:S(2)}, u32[]{:S(2)}) %all-to-all-start) | async-done | bytes 262176 | tf_op jit(solution)/shard_map/all_to_all | solution.py:13
  54.9 0.5 multiply_subtract_fusion
  56.6 0.9 %copy.21 = f32[2,8,2,2048]{3,2,1,0:T(2,128)} copy(f32[2,8,2,2048]{3,1,0,2:T(8,128)S(1)} %pad_maximum_fusion.1) | data formatting | bytes 524288
  (89 shorter events, 17.0 us)
Async XLA Ops:
  0.6 0.7 %copy-start.3 = (f32[2,1]{0,1:T(1,128)S(1)}, f32[2,1]{0,1:T(1,128)}, u32[]{:S(2)}) copy-start(f32[2,1]{0,1:T(1,128)} %param.8) | copy-start | bytes 28
  1.3 1.1 %copy-start = (f32[2,1,2,128,128]{4,3,2,1,0:T(8,128)S(1)}, f32[2,1,2,128,128]{4,3,2,1,0:T(8,128)}, u32[]{:S(2)}) copy-start(f32[2,1,2,128,128]{4,3,2,1,0:T(8,128)} %param.10) | copy-start | bytes 786436
  7.3 7.7 %collective-permute-start = (f32[1,2,128,128]{3,2,1,0:T(8,128)S(1)}, f32[1,2,128,128]{3,2,1,0:T(8,128)S(1)}, u32[]{:S(2)}, u32[]{:S(2)}) collective-permute-start(f32[1,2,128,128]{3,2,1,0:T(8,128)S(1)} %maximum_add_fusion.6), channel_id=1, source_target_pairs={{0,8},{8,16},{16,24},{1,9},{9,17},{17,25},{2,10},{10,18},{18,26},{... | collective-permute-start | bytes 393224 | tf_op jit(solution)/shard_map/while/body/eval_jaxpr/ppermute | solution.py:20
  16.9 6.9 %collective-permute-start = (f32[1,2,128,128]{3,2,1,0:T(8,128)S(1)}, f32[1,2,128,128]{3,2,1,0:T(8,128)S(1)}, u32[]{:S(2)}, u32[]{:S(2)}) collective-permute-start(f32[1,2,128,128]{3,2,1,0:T(8,128)S(1)} %maximum_add_fusion.6), channel_id=1, source_target_pairs={{0,8},{8,16},{16,24},{1,9},{9,17},{17,25},{2,10},{10,18},{18,26},{... | collective-permute-start | bytes 393224 | tf_op jit(solution)/shard_map/while/body/eval_jaxpr/ppermute | solution.py:20
  25.8 6.9 %collective-permute-start = (f32[1,2,128,128]{3,2,1,0:T(8,128)S(1)}, f32[1,2,128,128]{3,2,1,0:T(8,128)S(1)}, u32[]{:S(2)}, u32[]{:S(2)}) collective-permute-start(f32[1,2,128,128]{3,2,1,0:T(8,128)S(1)} %maximum_add_fusion.6), channel_id=1, source_target_pairs={{0,8},{8,16},{16,24},{1,9},{9,17},{17,25},{2,10},{10,18},{18,26},{... | collective-permute-start | bytes 393224 | tf_op jit(solution)/shard_map/while/body/eval_jaxpr/ppermute | solution.py:20
  36.7 0.7 %copy-start.2 = (f32[2,1,2,128,128]{4,3,2,1,0:T(8,128)}, f32[2,1,2,128,128]{4,3,2,1,0:T(8,128)S(1)}, u32[]{:S(2)}) copy-start(f32[2,1,2,128,128]{4,3,2,1,0:T(8,128)S(1)} %get-tuple-element.70) | copy-start | bytes 786436
  42.5 3.9 %copy-start.1 = (f32[2,8,2,2048]{3,2,1,0:T(2,128)S(1)}, f32[2,8,2,2048]{3,2,1,0:T(2,128)}, u32[]{:S(2)}) copy-start(f32[2,8,2,2048]{3,2,1,0:T(2,128)} %param.11) | copy-start | bytes 786436
  42.5 10.8 %all-to-all-start = ((f32[8,2,1,2,2048]{4,1,3,2,0:T(2,128)}), f32[8,2,1,2,2048]{4,1,3,2,0:T(2,128)S(1)}, u32[]{:S(2)}, u32[]{:S(2)}) async-start(f32[8,2,1,2,2048]{4,1,3,2,0:T(2,128)} %fusion.70), calls=%async_computation | async-start | bytes 524288 | tf_op jit(solution)/shard_map/all_to_all | solution.py:13
